TPU v7x, 32 devices: a whole 2x2x4 slice. The times are simulated.
32 devices in a mesh: groups: 2 (over y), span: 4 (over z), head: 4 (over x, core).
Axes of the slice: x: 2, y: 2, z: 4, core: 2. Of those that a mesh axis runs over, the one named last changes fastest.
Arguments:
- query_rows: bfloat16 [2048, 6144], P(('groups', 'span', 'head')), parts along dimension 0, may hold values from -6 to 6
- key_rows: bfloat16 [2048, 1024], P(('groups', 'span', 'head')), parts along dimension 0, may hold values from -6 to 6
- value_rows: bfloat16 [2048, 1024], P(('groups', 'span', 'head')), parts along dimension 0, may hold values from -6 to 6
- frame_counts: int32 [16], P('groups'), parts along dimension 0, may hold values from 1 to 4, as said below
- noise_levels: int32 [16], P('groups'), parts along dimension 0, may hold values from 0 to 63
- span_mask: int32 [16, 8], P('groups'), parts along dimension 0, may hold values from 0 to 1, as said below
- level_gate: bfloat16 [64, 6144], P(None, 'head'), may hold values from 0.19921875 to 1.796875
Outputs:
- attended: bfloat16 [2048, 6144], P(('groups', 'span', 'head')), parts along dimension 0
There are 2 independent parts, one for each index of `groups`. A program takes and returns all parts, laid end to end along the dimension named above; an argument that names none is the same for every part. Nothing has to cross between parts.
Inputs may be any that keep to these rules, and one draw needn't show every extreme that they name: `frame_counts`: each span holds at least one frame, and some span holds exactly 4. span_mask[c, c] = 1 for every span, span_mask[c, e] = 0 for e > c, entries below the diagonal are 0 or 1.
All inputs are finite; a program needn't handle non-finite values.
Results may differ from a plain program's by a relative error of at most 0.0033.
Values may be sent and summed in bfloat16 or wider, within the bound.
No kernel may reach another device: no remote copies, remote signals or barrier semaphores. Data moves between devices by JAX's collectives and lax.ppermute only.
A program may use at most 64 MiB of HBM per device.

v0:
```python
import math
import jax
import jax.numpy as jnp
from jax import lax
from jax.sharding import PartitionSpec as P

HD = 128
FRAME_TOK = 32
CT = 128
CH_DEV = 2


def attend(slot_state, query_block, key_piece, value_piece, usable, score_scale):
    run_max, run_sum, run_acc = slot_state
    scores = (
        jnp.einsum("qhgd,khd->hgqk", query_block, key_piece, preferred_element_type=jnp.float32)
        * score_scale
    )
    scores = jnp.where(usable[None, None, None, :], scores, -jnp.inf)
    new_max = jnp.maximum(run_max, jnp.max(scores, axis=3))
    weights = jnp.exp(scores - new_max[..., None])
    factor = jnp.exp(run_max - new_max)
    new_sum = factor * run_sum + jnp.sum(weights, axis=3)
    update = jnp.einsum(
        "hgqk,khd->qhgd",
        weights.astype(jnp.bfloat16),
        value_piece,
        preferred_element_type=jnp.float32,
    )
    new_acc = run_acc * jnp.transpose(factor, (2, 0, 1))[..., None] + update
    return (new_max, new_sum, new_acc)


def body(query_rows, key_rows, value_rows, frame_counts, noise_levels, span_mask, level_gate):
    q_local, k_local, v_local = (
        lax.all_to_all(query_rows, "head", split_axis=1, concat_axis=0, tiled=True),
        lax.all_to_all(key_rows, "head", split_axis=1, concat_axis=0, tiled=True),
        lax.all_to_all(value_rows, "head", split_axis=1, concat_axis=0, tiled=True),
    )
    span_devices = lax.axis_size("span")
    device_index = lax.axis_index("span")
    heads_dev = q_local.shape[1] // HD
    kv_dev = k_local.shape[1] // HD
    group_size = heads_dev // kv_dev
    score_scale = 1.0 / math.sqrt(HD)
    first_block = q_local[:CT]
    second_block = q_local[CT:]
    own_spans = jnp.stack([2 * device_index, 2 * device_index + 1])
    total_rows = CH_DEV * span_devices * CT
    position = jnp.arange(CT, dtype=jnp.int32)
    live_rows = position[None, :] < (frame_counts * FRAME_TOK)[:, None]
    live_flat = live_rows.reshape(-1)
    queries = jnp.stack([first_block, second_block]).reshape(2, CT, kv_dev, group_size, HD)
    allowed = []
    query_live = []
    gate_rows = []
    for member in range(2):
        mask_row = lax.dynamic_index_in_dim(span_mask, own_spans[member], 0, keepdims=False)
        allowed.append((jnp.repeat(mask_row, CT, total_repeat_length=total_rows) > 0) & live_flat)
        query_live.append(lax.dynamic_index_in_dim(live_rows, own_spans[member], 0, keepdims=False))
        level_index = lax.dynamic_index_in_dim(noise_levels, own_spans[member], 0, keepdims=False)
        gate_rows.append(
            lax.dynamic_index_in_dim(level_gate, level_index, 0, keepdims=False).astype(jnp.float32)
        )
    allowed = jnp.stack(allowed)

    def fold_step(running, kv_piece):
        key_piece, value_piece = kv_piece
        piece_rows = key_piece.shape[0]
        key_piece = key_piece.reshape(piece_rows, kv_dev, HD)
        value_piece = value_piece.reshape(piece_rows, kv_dev, HD)
        usable = lax.slice_in_dim(allowed, 0, piece_rows, axis=1)
        results = []
        for member in range(2):
            slot_state = (running[0][member], running[1][member], running[2][member])

            def compute(slot_state, member=member):
                return attend(
                    slot_state, queries[member], key_piece, value_piece, usable[member], score_scale
                )

            def keep_state(slot_state):
                return slot_state

            results.append(lax.cond(jnp.any(usable[member]), compute, keep_state, slot_state))
        return (
            jnp.stack([results[0][0], results[1][0]]),
            jnp.stack([results[0][1], results[1][1]]),
            jnp.stack([results[0][2], results[1][2]]),
        )

    initial = (
        jnp.full((2, kv_dev, group_size, CT), -1e30, jnp.float32),
        jnp.zeros((2, kv_dev, group_size, CT), jnp.float32),
        jnp.zeros((2, CT, kv_dev, group_size, HD), jnp.float32),
    )
    run_max, run_sum, run_acc = fold_step(
        initial,
        (
            lax.all_gather(k_local, "span", axis=0, tiled=True),
            lax.all_gather(v_local, "span", axis=0, tiled=True),
        ),
    )
    outputs = []
    for member in range(2):
        normed = run_acc[member] / jnp.transpose(run_sum[member], (2, 0, 1))[..., None]
        normed = normed.reshape(CT, heads_dev * HD) * gate_rows[member][None, :]
        outputs.append(
            jnp.where(query_live[member][:, None], normed, jnp.float32(0.0)).astype(jnp.bfloat16)
        )
    first_out = outputs[0]
    second_out = outputs[1]
    merged = jnp.concatenate([first_out, second_out], axis=0)
    return lax.all_to_all(merged, "head", split_axis=0, concat_axis=1, tiled=True)


def solution(mesh):
    placed = (
        P(("groups", "span", "head"), None),
        P(("groups", "span", "head"), None),
        P(("groups", "span", "head"), None),
        P("groups"),
        P("groups"),
        P("groups", None),
        P(None, "head"),
    )
    return jax.shard_map(
        body,
        mesh=mesh,
        in_specs=placed,
        out_specs=P(("groups", "span", "head"), None),
        check_vma=False,
    )
```

profile of v0, /device:TPU:0, one launch (start us, length us, event | category | flops | bytes accessed | tf_op | source)
XLA Modules:
  0.0 101.1 jit_solution(4558437299421896229)
XLA Ops:
  0.0 1.6 %copy.85 = bf16[8,4,8,256]{3,2,0,1:T(8,128)(2,1)} copy(bf16[8,4,8,256]{3,2,1,0:T(8,128)(2,1)} %bitcast.212) | data formatting | bytes 262144 | tf_op jit(solution)/shard_map/all_to_all | solution.py:37
  1.6 4.2 %all-to-all-start.1 = ((bf16[64,4,256]{2,0,1:T(8,128)(2,1)}), bf16[64,4,256]{2,0,1:T(8,128)(2,1)S(1)}, u32[]{:S(2)}, u32[]{:S(2)}) async-start(bf16[64,4,256]{2,0,1:T(8,128)(2,1)} %bitcast.201), calls=%async_computation.1 | async-start | bytes 262144 | tf_op jit(solution)/shard_map/all_to_all | solution.py:37
  6.5 1.5 %copy.84 = bf16[8,4,8,256]{3,2,0,1:T(8,128)(2,1)} copy(bf16[8,4,8,256]{3,2,1,0:T(8,128)(2,1)} %bitcast.213) | data formatting | bytes 262144 | tf_op jit(solution)/shard_map/all_to_all | solution.py:38
  8.0 0.8 fusion.52
  9.5 0.9 all-to-all-done.1
  10.4 3.3 %all-to-all-start.2 = ((bf16[64,4,256]{2,0,1:T(8,128)(2,1)}), bf16[64,4,256]{2,0,1:T(8,128)(2,1)S(1)}, u32[]{:S(2)}, u32[]{:S(2)}) async-start(bf16[64,4,256]{2,0,1:T(8,128)(2,1)} %bitcast.200), calls=%async_computation.2 | async-start | bytes 262144 | tf_op jit(solution)/shard_map/all_to_all | solution.py:38
  13.7 10.7 %fusion.54 = (pred[]{:T(512)}, pred[1024]{0:T(1024)(128)(4,1)S(1)}, pred[]{:T(512)}, pred[1024]{0:T(1024)(128)(4,1)S(1)}) fusion(s32[8]{0:T(128)S(1)} %broadcast_multiply_fusion, s32[]{:T(128)} %bitcast.22, s32[]{:T(128)} %bitcast.21, s32[]{:T(128)} %bitcast.20, s32[]{:T(128)} %bitcast.19, s32[]{:T(128)} %bitcast.18, s32[]{:T(128)} %bitcast.17, s32[]{:T(128)} %bitcast.16, ...), kind=kLoop, calls=%fused_computation.79 | loop fusion | flops 38910 | bytes 2146 | tf_op jit(solution)/shard_map/reduce_or | solution.py:85
  24.4 2.1 %copy.83 = bf16[8,4,8,1536]{3,2,0,1:T(8,128)(2,1)} copy(bf16[8,4,8,1536]{3,2,1,0:T(8,128)(2,1)} %bitcast.207) | data formatting | bytes 1572864 | tf_op jit(solution)/shard_map/all_to_all | solution.py:36
  26.5 3.5 %all-to-all-start = ((bf16[64,4,1536]{2,0,1:T(8,128)(2,1)}), bf16[64,4,1536]{2,0,1:T(8,128)(2,1)S(1)}, u32[]{:S(2)}, u32[]{:S(2)}) async-start(bf16[64,4,1536]{2,0,1:T(8,128)(2,1)} %bitcast.199), calls=%async_computation | async-start | bytes 1572864 | tf_op jit(solution)/shard_map/all_to_all | solution.py:36
  30.1 1.4 %fusion.58 = (s32[1]{0:T(128)}, s32[1]{0:T(128)}) fusion(s32[8]{0:T(128)} %param.21, s32[]{:T(128)S(6)} %select_n.53, s32[]{:T(128)S(6)} %select_n.50), kind=kLoop, calls=%fused_computation.83 | loop fusion | bytes 24 | tf_op jit(solution)/shard_map/jit(dynamic_index_in_dim)/dynamic_slice | solution.py:61
  36.5 0.8 convert_reduce_fusion.1
  37.3 17.0 %all_gather.7 = bf16[1024,256]{1,0:T(8,128)(2,1)S(1)} all-gather(bf16[256,256]{1,0:T(8,128)(2,1)S(1)} %bitcast.209), channel_id=1, replica_groups=mesh['groups'=2,'span'=4,'head'=4] {'span'}, dimensions={0}, use_global_device_ids=true | all-gather | bytes 655360 | tf_op jit(solution)/shard_map/all_gather | solution.py:101
  54.3 1.0 copy.47
  55.3 16.0 %all_gather.6 = bf16[1024,256]{1,0:T(8,128)(2,1)S(1)} all-gather(bf16[256,256]{1,0:T(8,128)(2,1)S(1)} %bitcast.208), channel_id=1, replica_groups=mesh['groups'=2,'span'=4,'head'=4] {'span'}, dimensions={0}, use_global_device_ids=true | all-gather | bytes 655360 | tf_op jit(solution)/shard_map/all_gather | solution.py:100
  72.7 5.9 %conditional.2 = (f32[2,6,128]{2,1,0:T(8,128)S(1)}, f32[128,2,6,128]{0,3,2,1:T(8,128)S(1)}) conditional(s32[]{:T(128)} %convert_element_type.22, () %tuple.29, (pred[1024]{0:T(1024)(128)(4,1)S(1)}, bf16[2,128,2,6,128]{4,3,2,1,0:T(8,128)(2,1)S(1)}, bf16[1024,2,128]{0,2,1:T(8,128)(2,1)S(1)}, bf16[1024,2,128]{0,2,1:T(8,128)(2,1)}) %tuple.84), branch_computations={%region_1.3_spmd, %region_2.6_spmd} | conditional | flops 822809088 | bytes 26416172 | solution.py:85
  73.0 1.5 %bitcast_reduce_fusion = (f32[2,6,128]{2,1,0:T(8,128)S(1)}, f32[2,1024,128,6]{2,1,3,0:T(8,128)S(1)}) fusion(pred[1024]{0:T(1024)(128)(4,1)S(1)} %get-tuple-element.42, bf16[2,128,2,6,128]{4,1,3,2,0:T(8,128)(2,1)S(1)} %copy.48, bf16[1024,2,128]{0,2,1:T(8,128)(2,1)S(1)} %get-tuple-element.76), kind=kOutput, calls=%fused_computation.1 | convolution fusion | flops 407370240 | bytes 7216128 | tf_op jit(solution)/shard_map/cond/branch_1_fun/qhgd,khd->hgqk/dot_general | solution.py:16
  74.5 1.8 %fusion.2 = f32[2,6,128]{2,1,0:T(8,128)S(1)} fusion(f32[2,1024,128,6]{2,1,3,0:T(8,128)S(1)} %get-tuple-element.93, f32[2,6,128]{2,1,0:T(8,128)S(1)} %broadcast_maximum_fusion, pred[1024]{0:T(1024)(128)(4,1)S(1)} %get-tuple-element.42), kind=kLoop, calls=%fused_computation.5 | loop fusion | flops 6289920 | bytes 6304768 | tf_op jit(solution)/shard_map/cond/branch_1_fun/reduce_sum | solution.py:23
  76.3 2.1 %fusion.9 = f32[128,2,6,128]{3,0,2,1:T(8,128)S(1)} fusion(f32[2,1024,128,6]{2,1,3,0:T(8,128)S(1)} %get-tuple-element.93, f32[2,6,128]{2,1,0:T(8,128)S(1)} %broadcast_maximum_fusion, pred[1024]{0:T(1024)(128)(4,1)S(1)} %get-tuple-element.42, bf16[1024,2,128]{0,2,1:T(8,128)(2,1)S(1)} %copy-done, f32[128,2,6]{0,2,1:T(8,128)S(1)} %get-tuple-element.90), kind=kOutput, calls=%fused_computation.9 | convolution fusion | flops 409141248 | bytes 7615488 | tf_op jit(solution)/shard_map/cond/branch_1_fun/hgqk,khd->qhgd/dot_general | solution.py:24
  78.7 6.0 %conditional.3 = (f32[2,6,128]{2,1,0:T(8,128)S(1)}, f32[128,2,6,128]{0,3,2,1:T(8,128)S(1)}) conditional(s32[]{:T(128)} %convert_element_type.24, () %tuple.31, (pred[1024]{0:T(1024)(128)(4,1)S(1)}, bf16[2,128,2,6,128]{4,3,2,1,0:T(8,128)(2,1)S(1)}, bf16[1024,2,128]{0,2,1:T(8,128)(2,1)S(1)}, bf16[1024,2,128]{0,2,1:T(8,128)(2,1)}) %tuple.85), branch_computations={%region_6.8_spmd, %region_7.11_spmd} | conditional | flops 822809088 | bytes 26416172 | solution.py:85
  79.1 1.5 %bitcast_reduce_fusion.1 = (f32[2,6,128]{2,1,0:T(8,128)S(1)}, f32[2,1024,128,6]{2,1,3,0:T(8,128)S(1)}) fusion(pred[1024]{0:T(1024)(128)(4,1)S(1)} %get-tuple-element.46, bf16[2,128,2,6,128]{4,1,3,2,0:T(8,128)(2,1)S(1)} %copy.52, bf16[1024,2,128]{0,2,1:T(8,128)(2,1)S(1)} %get-tuple-element.80), kind=kOutput, calls=%fused_computation.21 | convolution fusion | flops 407370240 | bytes 7216128 | tf_op jit(solution)/shard_map/cond/branch_1_fun/qhgd,khd->hgqk/dot_general | solution.py:16
  80.6 1.8 %fusion.21 = f32[2,6,128]{2,1,0:T(8,128)S(1)} fusion(f32[2,1024,128,6]{2,1,3,0:T(8,128)S(1)} %get-tuple-element.97, f32[2,6,128]{2,1,0:T(8,128)S(1)} %broadcast_maximum_fusion.1, pred[1024]{0:T(1024)(128)(4,1)S(1)} %get-tuple-element.46), kind=kLoop, calls=%fused_computation.25 | loop fusion | flops 6289920 | bytes 6304768 | tf_op jit(solution)/shard_map/cond/branch_1_fun/reduce_sum | solution.py:23
  82.4 2.1 %fusion.28 = f32[128,2,6,128]{3,0,2,1:T(8,128)S(1)} fusion(f32[2,1024,128,6]{2,1,3,0:T(8,128)S(1)} %get-tuple-element.97, f32[2,6,128]{2,1,0:T(8,128)S(1)} %broadcast_maximum_fusion.1, pred[1024]{0:T(1024)(128)(4,1)S(1)} %get-tuple-element.46, bf16[1024,2,128]{0,2,1:T(8,128)(2,1)S(1)} %copy-done.1, f32[128,2,6]{0,2,1:T(8,128)S(1)} %get-tuple-element.94), kind=kOutput, calls=%fused_computation.29 | convolution fusion | flops 409141248 | bytes 7615488 | tf_op jit(solution)/shard_map/cond/branch_1_fun/hgqk,khd->qhgd/dot_general | solution.py:24
  85.7 14.4 %all_to_all.73 = bf16[4,64,1536]{2,1,0:T(8,128)(2,1)S(1)} all-to-all(bf16[4,64,1536]{2,1,0:T(8,128)(2,1)S(1)} %bitcast.205), channel_id=1, replica_groups=mesh['groups'=2,'span'=4,'head'=4] {'head'}, dimensions={0} | all-to-all | bytes 1572864 | tf_op jit(solution)/shard_map/all_to_all | solution.py:114
  100.1 0.9 copy.79
  (30 shorter events, 4.8 us)
Async XLA Ops:
  1.6 8.8 %all-to-all-start.1 = ((bf16[64,4,256]{2,0,1:T(8,128)(2,1)}), bf16[64,4,256]{2,0,1:T(8,128)(2,1)S(1)}, u32[]{:S(2)}, u32[]{:S(2)}) async-start(bf16[64,4,256]{2,0,1:T(8,128)(2,1)} %bitcast.201), calls=%async_computation.1 | async-start | bytes 262144 | tf_op jit(solution)/shard_map/all_to_all | solution.py:37
  10.4 16.1 %all-to-all-start.2 = ((bf16[64,4,256]{2,0,1:T(8,128)(2,1)}), bf16[64,4,256]{2,0,1:T(8,128)(2,1)S(1)}, u32[]{:S(2)}, u32[]{:S(2)}) async-start(bf16[64,4,256]{2,0,1:T(8,128)(2,1)} %bitcast.200), calls=%async_computation.2 | async-start | bytes 262144 | tf_op jit(solution)/shard_map/all_to_all | solution.py:38
  26.5 45.0 %all-to-all-start = ((bf16[64,4,1536]{2,0,1:T(8,128)(2,1)}), bf16[64,4,1536]{2,0,1:T(8,128)(2,1)S(1)}, u32[]{:S(2)}, u32[]{:S(2)}) async-start(bf16[64,4,1536]{2,0,1:T(8,128)(2,1)} %bitcast.199), calls=%async_computation | async-start | bytes 1572864 | tf_op jit(solution)/shard_map/all_to_all | solution.py:36
  73.0 3.3 %copy-start = (bf16[1024,2,128]{0,2,1:T(8,128)(2,1)S(1)}, bf16[1024,2,128]{0,2,1:T(8,128)(2,1)}, u32[]{:S(2)}) copy-start(bf16[1024,2,128]{0,2,1:T(8,128)(2,1)} %get-tuple-element.77) | copy-start | bytes 1572868 | tf_op jit(solution)/shard_map/cond
  79.1 3.3 %copy-start.1 = (bf16[1024,2,128]{0,2,1:T(8,128)(2,1)S(1)}, bf16[1024,2,128]{0,2,1:T(8,128)(2,1)}, u32[]{:S(2)}) copy-start(bf16[1024,2,128]{0,2,1:T(8,128)(2,1)} %get-tuple-element.81) | copy-start | bytes 1572868 | tf_op jit(solution)/shard_map/cond
where the time goes:
time: 102 us; the launch traced here: 101 us
  blocking collectives  47.4 us (46%)
  other arithmetic  16.6 us (16%)
  local copies, waits for them, and re-layouts  12.6 us (12%)
  starting transfers between devices  11.1 us (11%)
  matrix products  7.04 us (7%)
  between operations  5.14 us (5%)
    all_gather x1, blocking collectives, body(): lax.all_gather(v_local, 'span', axis=0, tiled=True)  17 us
    all_gather x1, blocking collectives, body(): lax.all_gather(k_local, 'span', axis=0, tiled=True)  16 us
    all_to_all x1, blocking collectives, body(): lax.all_to_all(merged, 'head', split_axis=0, concat_axis=1, tiled=True)  14.4 us
    reduce_or x1, other arithmetic, fold_step(): jnp.any(usable[member])  10.7 us
    all_to_all x1, starting transfers between devices, body(): lax.all_to_all(key_rows, 'head', split_axis=1, concat_axis=0, tiled=True)  4.24 us
    dot_general x2, matrix products, attend(): jnp.einsum('hgqk,khd->qhgd', weights.astype(jnp.bfloat16), value_piece, p...  4.1 us
    reduce_sum x2, other arithmetic, attend(): new_sum = factor * run_sum + jnp.sum(weights, axis=3)  3.54 us
    all_to_all x1, starting transfers between devices, body(): lax.all_to_all(query_rows, 'head', split_axis=1, concat_axis=0, tiled=True)  3.5 us
  transfers between devices with their start and end apart: 3, of which 1 were waited for; matrix products, arithmetic and copies ran while one was open for 20% of the time, Pallas kernels for 0%

commit v1 on v0

--- a/solution.py
+++ b/solution.py
@@ -8,6 +8,12 @@
 FRAME_TOK = 32
 CT = 128
 CH_DEV = 2
+
+
+def exchange_blocks(value, name, split, join):
+    parts = jnp.split(value, lax.axis_size(name), axis=split)
+    got = lax.all_to_all(jnp.stack(parts), name, 0, 0)
+    return jnp.concatenate(got, axis=join)
 
 
 def attend(slot_state, query_block, key_piece, value_piece, usable, score_scale):
@@ -34,7 +40,7 @@
 def body(query_rows, key_rows, value_rows, frame_counts, noise_levels, span_mask, level_gate):
     q_local, k_local, v_local = (
         lax.all_to_all(query_rows, "head", split_axis=1, concat_axis=0, tiled=True),
-        lax.all_to_all(key_rows, "head", split_axis=1, concat_axis=0, tiled=True),
+        exchange_blocks(key_rows, "head", 1, 0),
         lax.all_to_all(value_rows, "head", split_axis=1, concat_axis=0, tiled=True),
     )
     span_devices = lax.axis_size("span")

time: 102 us -> 102 us (level)
    all_to_all x1 -> x0, local copies, waits for them, and re-layouts: 1.57 us -> none  [body(): lax.all_to_all(key_rows, 'head', split_axis=1, concat_axis=0, tiled=True)]
where the time goes in v1:
time: 102 us; the launch traced here: 101 us
  blocking collectives  47.4 us (46%)
  other arithmetic  17.3 us (17%)
  local copies, waits for them, and re-layouts  11.9 us (12%)
  starting transfers between devices  11.1 us (11%)
  matrix products  7.03 us (7%)
  between operations  5.04 us (5%)
    all_gather x1, blocking collectives, body(): lax.all_gather(k_local, 'span', axis=0, tiled=True)  17 us
    all_gather x1, blocking collectives, body(): lax.all_gather(v_local, 'span', axis=0, tiled=True)  16 us
    all_to_all x1, blocking collectives, body(): lax.all_to_all(merged, 'head', split_axis=0, concat_axis=1, tiled=True)  14.4 us
    reduce_or x1, other arithmetic, fold_step(): jnp.any(usable[member])  10.8 us
    all_to_all x1, starting transfers between devices, body(): lax.all_to_all(value_rows, 'head', split_axis=1, concat_axis=0, tiled=True)  4.24 us
    dot_general x2, matrix products, attend(): jnp.einsum('hgqk,khd->qhgd', weights.astype(jnp.bfloat16), value_piece, p...  4.1 us
    reduce_sum x2, other arithmetic, attend(): new_sum = factor * run_sum + jnp.sum(weights, axis=3)  3.54 us
    all_to_all x1, starting transfers between devices, body(): lax.all_to_all(query_rows, 'head', split_axis=1, concat_axis=0, tiled=True)  3.5 us
  transfers between devices with their start and end apart: 3, of which 1 were waited for; matrix products, arithmetic and copies ran while one was open for 20% of the time, Pallas kernels for 0%

profile of v1, /device:TPU:0, one launch (start us, length us, event | category | flops | bytes accessed | tf_op | source)
XLA Modules:
  0.0 101.0 jit_solution(2970483900391583913)
XLA Ops:
  0.0 1.6 %copy.80 = bf16[8,4,8,256]{3,2,0,1:T(8,128)(2,1)} copy(bf16[8,4,8,256]{3,2,1,0:T(8,128)(2,1)} %bitcast.214) | data formatting | bytes 262144 | tf_op jit(solution)/shard_map/all_to_all | solution.py:44
  1.6 4.2 %all-to-all-start.2 = ((bf16[64,4,256]{2,0,1:T(8,128)(2,1)}), bf16[64,4,256]{2,0,1:T(8,128)(2,1)S(1)}, u32[]{:S(2)}, u32[]{:S(2)}) async-start(bf16[64,4,256]{2,0,1:T(8,128)(2,1)} %bitcast.203), calls=%async_computation.2 | async-start | bytes 262144 | tf_op jit(solution)/shard_map/all_to_all | solution.py:44
  6.5 0.8 slice_bitcast_fusion.7
  7.3 0.8 fusion.52
  9.4 1.0 all-to-all-done.2
  10.4 3.3 %all-to-all-start.1 = ((bf16[4,64,256]{2,1,0:T(8,128)(2,1)}), bf16[4,64,256]{2,1,0:T(8,128)(2,1)S(1)}, u32[]{:S(2)}, u32[]{:S(2)}) async-start(bf16[4,64,256]{2,1,0:T(8,128)(2,1)} %pad_maximum_fusion.1), calls=%async_computation.1 | async-start | bytes 262144 | tf_op jit(solution)/shard_map/all_to_all | solution.py:15
  13.7 10.8 %fusion.54 = (pred[]{:T(512)}, pred[1024]{0:T(1024)(128)(4,1)S(1)}, pred[]{:T(512)}, pred[1024]{0:T(1024)(128)(4,1)S(1)}) fusion(s32[8]{0:T(128)S(1)} %broadcast_multiply_fusion, s32[]{:T(128)} %bitcast.22, s32[]{:T(128)} %bitcast.21, s32[]{:T(128)} %bitcast.20, s32[]{:T(128)} %bitcast.19, s32[]{:T(128)} %bitcast.18, s32[]{:T(128)} %bitcast.17, s32[]{:T(128)} %bitcast.16, ...), kind=kLoop, calls=%fused_computation.83 | loop fusion | flops 38910 | bytes 2146 | tf_op jit(solution)/shard_map/reduce_or | solution.py:91
  24.5 2.1 %copy.79 = bf16[8,4,8,1536]{3,2,0,1:T(8,128)(2,1)} copy(bf16[8,4,8,1536]{3,2,1,0:T(8,128)(2,1)} %bitcast.209) | data formatting | bytes 1572864 | tf_op jit(solution)/shard_map/all_to_all | solution.py:42
  26.6 3.5 %all-to-all-start = ((bf16[64,4,1536]{2,0,1:T(8,128)(2,1)}), bf16[64,4,1536]{2,0,1:T(8,128)(2,1)S(1)}, u32[]{:S(2)}, u32[]{:S(2)}) async-start(bf16[64,4,1536]{2,0,1:T(8,128)(2,1)} %bitcast.202), calls=%async_computation | async-start | bytes 1572864 | tf_op jit(solution)/shard_map/all_to_all | solution.py:42
  30.1 1.3 %fusion.58 = (s32[1]{0:T(128)}, s32[1]{0:T(128)}) fusion(s32[8]{0:T(128)} %param.21, s32[]{:T(128)S(6)} %select_n.53, s32[]{:T(128)S(6)} %select_n.50), kind=kLoop, calls=%fused_computation.87 | loop fusion | bytes 24 | tf_op jit(solution)/shard_map/jit(dynamic_index_in_dim)/dynamic_slice | solution.py:67
  36.4 0.8 convert_reduce_fusion.1
  37.2 17.0 %all_gather.6 = bf16[1024,256]{1,0:T(8,128)(2,1)S(1)} all-gather(bf16[256,256]{1,0:T(8,128)(2,1)S(1)} %bitcast.211), channel_id=1, replica_groups=mesh['groups'=2,'span'=4,'head'=4] {'span'}, dimensions={0}, use_global_device_ids=true | all-gather | bytes 655360 | tf_op jit(solution)/shard_map/all_gather | solution.py:106
  54.4 16.0 %all_gather.7 = bf16[1024,256]{1,0:T(8,128)(2,1)S(1)} all-gather(bf16[256,256]{1,0:T(8,128)(2,1)S(1)} %bitcast.210), channel_id=1, replica_groups=mesh['groups'=2,'span'=4,'head'=4] {'span'}, dimensions={0}, use_global_device_ids=true | all-gather | bytes 655360 | tf_op jit(solution)/shard_map/all_gather | solution.py:107
  70.4 1.0 copy.45
  72.7 5.9 %conditional.2 = (f32[2,6,128]{2,1,0:T(8,128)S(1)}, f32[128,2,6,128]{0,3,2,1:T(8,128)S(1)}) conditional(s32[]{:T(128)} %convert_element_type.22, () %tuple.29, (pred[1024]{0:T(1024)(128)(4,1)S(1)}, bf16[2,128,2,6,128]{4,3,2,1,0:T(8,128)(2,1)S(1)}, bf16[1024,2,128]{0,2,1:T(8,128)(2,1)S(1)}, bf16[1024,2,128]{0,2,1:T(8,128)(2,1)}) %tuple.87), branch_computations={%region_1.3_spmd, %region_2.6_spmd} | conditional | flops 822809088 | bytes 26416172 | solution.py:91
  72.9 1.5 %bitcast_reduce_fusion = (f32[2,6,128]{2,1,0:T(8,128)S(1)}, f32[2,1024,128,6]{2,1,3,0:T(8,128)S(1)}) fusion(pred[1024]{0:T(1024)(128)(4,1)S(1)} %get-tuple-element.42, bf16[2,128,2,6,128]{4,1,3,2,0:T(8,128)(2,1)S(1)} %copy.46, bf16[1024,2,128]{0,2,1:T(8,128)(2,1)S(1)} %get-tuple-element.76), kind=kOutput, calls=%fused_computation.1 | convolution fusion | flops 407370240 | bytes 7216128 | tf_op jit(solution)/shard_map/cond/branch_1_fun/qhgd,khd->hgqk/dot_general | solution.py:22
  74.4 1.8 %fusion.2 = f32[2,6,128]{2,1,0:T(8,128)S(1)} fusion(f32[2,1024,128,6]{2,1,3,0:T(8,128)S(1)} %get-tuple-element.93, f32[2,6,128]{2,1,0:T(8,128)S(1)} %broadcast_maximum_fusion, pred[1024]{0:T(1024)(128)(4,1)S(1)} %get-tuple-element.42), kind=kLoop, calls=%fused_computation.5 | loop fusion | flops 6289920 | bytes 6304768 | tf_op jit(solution)/shard_map/cond/branch_1_fun/reduce_sum | solution.py:29
  76.2 2.0 %fusion.9 = f32[128,2,6,128]{3,0,2,1:T(8,128)S(1)} fusion(f32[2,1024,128,6]{2,1,3,0:T(8,128)S(1)} %get-tuple-element.93, f32[2,6,128]{2,1,0:T(8,128)S(1)} %broadcast_maximum_fusion, pred[1024]{0:T(1024)(128)(4,1)S(1)} %get-tuple-element.42, bf16[1024,2,128]{0,2,1:T(8,128)(2,1)S(1)} %copy-done, f32[128,2,6]{0,2,1:T(8,128)S(1)} %get-tuple-element.90), kind=kOutput, calls=%fused_computation.9 | convolution fusion | flops 409141248 | bytes 7615488 | tf_op jit(solution)/shard_map/cond/branch_1_fun/hgqk,khd->qhgd/dot_general | solution.py:30
  78.6 6.0 %conditional.3 = (f32[2,6,128]{2,1,0:T(8,128)S(1)}, f32[128,2,6,128]{0,3,2,1:T(8,128)S(1)}) conditional(s32[]{:T(128)} %convert_element_type.24, () %tuple.31, (pred[1024]{0:T(1024)(128)(4,1)S(1)}, bf16[2,128,2,6,128]{4,3,2,1,0:T(8,128)(2,1)S(1)}, bf16[1024,2,128]{0,2,1:T(8,128)(2,1)S(1)}, bf16[1024,2,128]{0,2,1:T(8,128)(2,1)}) %tuple.88), branch_computations={%region_6.8_spmd, %region_7.11_spmd} | conditional | flops 822809088 | bytes 26416172 | solution.py:91
  79.0 1.5 %bitcast_reduce_fusion.1 = (f32[2,6,128]{2,1,0:T(8,128)S(1)}, f32[2,1024,128,6]{2,1,3,0:T(8,128)S(1)}) fusion(pred[1024]{0:T(1024)(128)(4,1)S(1)} %get-tuple-element.46, bf16[2,128,2,6,128]{4,1,3,2,0:T(8,128)(2,1)S(1)} %copy.50, bf16[1024,2,128]{0,2,1:T(8,128)(2,1)S(1)} %get-tuple-element.80), kind=kOutput, calls=%fused_computation.21 | convolution fusion | flops 407370240 | bytes 7216128 | tf_op jit(solution)/shard_map/cond/branch_1_fun/qhgd,khd->hgqk/dot_general | solution.py:22
  80.5 1.8 %fusion.21 = f32[2,6,128]{2,1,0:T(8,128)S(1)} fusion(f32[2,1024,128,6]{2,1,3,0:T(8,128)S(1)} %get-tuple-element.97, f32[2,6,128]{2,1,0:T(8,128)S(1)} %broadcast_maximum_fusion.1, pred[1024]{0:T(1024)(128)(4,1)S(1)} %get-tuple-element.46), kind=kLoop, calls=%fused_computation.25 | loop fusion | flops 6289920 | bytes 6304768 | tf_op jit(solution)/shard_map/cond/branch_1_fun/reduce_sum | solution.py:29
  82.3 2.1 %fusion.28 = f32[128,2,6,128]{3,0,2,1:T(8,128)S(1)} fusion(f32[2,1024,128,6]{2,1,3,0:T(8,128)S(1)} %get-tuple-element.97, f32[2,6,128]{2,1,0:T(8,128)S(1)} %broadcast_maximum_fusion.1, pred[1024]{0:T(1024)(128)(4,1)S(1)} %get-tuple-element.46, bf16[1024,2,128]{0,2,1:T(8,128)(2,1)S(1)} %copy-done.1, f32[128,2,6]{0,2,1:T(8,128)S(1)} %get-tuple-element.94), kind=kOutput, calls=%fused_computation.29 | convolution fusion | flops 409141248 | bytes 7615488 | tf_op jit(solution)/shard_map/cond/branch_1_fun/hgqk,khd->qhgd/dot_general | solution.py:30
  85.6 14.4 %all_to_all.59 = bf16[4,64,1536]{2,1,0:T(8,128)(2,1)S(1)} all-to-all(bf16[4,64,1536]{2,1,0:T(8,128)(2,1)S(1)} %bitcast.207), channel_id=1, replica_groups=mesh['groups'=2,'span'=4,'head'=4] {'head'}, dimensions={0} | all-to-all | bytes 1572864 | tf_op jit(solution)/shard_map/all_to_all | solution.py:120
  100.1 0.9 copy.76
  (31 shorter events, 5.5 us)
Async XLA Ops:
  1.6 8.8 %all-to-all-start.2 = ((bf16[64,4,256]{2,0,1:T(8,128)(2,1)}), bf16[64,4,256]{2,0,1:T(8,128)(2,1)S(1)}, u32[]{:S(2)}, u32[]{:S(2)}) async-start(bf16[64,4,256]{2,0,1:T(8,128)(2,1)} %bitcast.203), calls=%async_computation.2 | async-start | bytes 262144 | tf_op jit(solution)/shard_map/all_to_all | solution.py:44
  10.4 16.2 %all-to-all-start.1 = ((bf16[4,64,256]{2,1,0:T(8,128)(2,1)}), bf16[4,64,256]{2,1,0:T(8,128)(2,1)S(1)}, u32[]{:S(2)}, u32[]{:S(2)}) async-start(bf16[4,64,256]{2,1,0:T(8,128)(2,1)} %pad_maximum_fusion.1), calls=%async_computation.1 | async-start | bytes 262144 | tf_op jit(solution)/shard_map/all_to_all | solution.py:15
  26.6 44.9 %all-to-all-start = ((bf16[64,4,1536]{2,0,1:T(8,128)(2,1)}), bf16[64,4,1536]{2,0,1:T(8,128)(2,1)S(1)}, u32[]{:S(2)}, u32[]{:S(2)}) async-start(bf16[64,4,1536]{2,0,1:T(8,128)(2,1)} %bitcast.202), calls=%async_computation | async-start | bytes 1572864 | tf_op jit(solution)/shard_map/all_to_all | solution.py:42
  72.9 3.3 %copy-start = (bf16[1024,2,128]{0,2,1:T(8,128)(2,1)S(1)}, bf16[1024,2,128]{0,2,1:T(8,128)(2,1)}, u32[]{:S(2)}) copy-start(bf16[1024,2,128]{0,2,1:T(8,128)(2,1)} %get-tuple-element.77) | copy-start | bytes 1572868 | tf_op jit(solution)/shard_map/cond
  79.0 3.3 %copy-start.1 = (bf16[1024,2,128]{0,2,1:T(8,128)(2,1)S(1)}, bf16[1024,2,128]{0,2,1:T(8,128)(2,1)}, u32[]{:S(2)}) copy-start(bf16[1024,2,128]{0,2,1:T(8,128)(2,1)} %get-tuple-element.81) | copy-start | bytes 1572868 | tf_op jit(solution)/shard_map/cond
